TPU v7x, 512 devices: a whole 4x8x8 slice. The times are simulated.
512 devices in a mesh: rows: 32 (over x, z), cols: 16 (over y, core).
Axes of the slice: x: 4, y: 8, z: 8, core: 2. Of those that a mesh axis runs over, the one named last changes fastest.
Arguments:
- targets: float32 [3, 65536], P(None, 'rows'), may hold values from 0 to 1
- sources: float32 [3, 65536], P(None, 'cols'), may hold values from 0 to 1
- weights: float32 [65536], P('cols'), may hold values from 0.5 to 2
- counts: int32 [4096], P('cols'), may hold values from 8 to 16, as said below
- omega: bfloat16 [65536, 128], P('cols'), may hold values from -0.0234375 to 0.0234375
Outputs:
- basis: float32 [65536, 128], P('rows')
- projected: float32 [65536, 128], P(('cols', 'rows'))
Inputs may be any that keep to these rules, and one draw needn't show every extreme that they name: `counts`: some panel uses all 16 nodes.
All inputs are finite; a program needn't handle non-finite values.
Results may differ from a plain program's by a relative error of at most 0.0033.
Values may be sent and summed in bfloat16 or wider, within the bound.
No kernel may reach another device: no remote copies, remote signals or barrier semaphores. Data moves between devices by JAX's collectives and lax.ppermute only.
A program may use at most 64 MiB of HBM per device.

v0:
```python
import math
import jax
import jax.numpy as jnp
from jax import lax
from jax.sharding import PartitionSpec as P

wave_number = 160.0
separation = 2.0


def kernel_cols(targets, src_block, wts_block):
    diff_x = targets[0][None, :] - (src_block[0][:, None] + separation)
    diff_y = targets[1][None, :] - src_block[1][:, None]
    diff_z = targets[2][None, :] - src_block[2][:, None]
    distance = jnp.sqrt(diff_x * diff_x + diff_y * diff_y + diff_z * diff_z)
    return (wts_block[:, None] * jnp.cos(wave_number * distance) / distance).astype(jnp.bfloat16)


def contract_first(left, right):
    return lax.dot_general(
        left, right, (((0,), (0,)), ((), ())), preferred_element_type=jnp.float32
    )


def gram_of(rows_block):
    return jnp.dot(
        rows_block.T,
        rows_block,
        precision=lax.Precision.HIGHEST,
        preferred_element_type=jnp.float32,
    )


def solve_rows(rows_block, gram_matrix):
    lower_factor = jnp.linalg.cholesky(gram_matrix)
    return lax.linalg.triangular_solve(
        lower_factor, rows_block, left_side=False, lower=True, transpose_a=True
    )


def shards(targets, sources, weights, counts, omega):
    rows_here = targets.shape[1]
    cols_here = sources.shape[1]
    rank = omega.shape[1]
    panel_count = counts.shape[0]
    panel_size = cols_here // panel_count
    usable = (
        (lax.broadcasted_iota(jnp.int32, (panel_count, panel_size), 1) < counts[:, None])
        .reshape(-1)
        .astype(jnp.float32)
    )
    node_weight = weights * usable
    block_width = math.gcd(cols_here, 512)
    nblocks = cols_here // block_width
    src_blocks = sources.reshape(3, nblocks, block_width).transpose(1, 0, 2)
    wts_blocks = node_weight.reshape(nblocks, block_width)
    omega_blocks = omega.reshape(nblocks, block_width, rank)

    def sketch_turn(total, inputs):
        kernel_tile = kernel_cols(targets, inputs[0], inputs[1])
        return (total + contract_first(kernel_tile, inputs[2]), None)

    partial_sketch, _ = lax.scan(
        sketch_turn,
        jnp.zeros((rows_here, rank), jnp.float32),
        (src_blocks, wts_blocks, omega_blocks),
    )
    sketch = lax.psum(partial_sketch, "cols")
    gram_matrix = lax.psum(gram_of(sketch), "rows")
    ortho = solve_rows(sketch, gram_matrix)
    ortho_low = ortho.astype(jnp.bfloat16)
    row_devices = lax.axis_size("rows")
    own_count = cols_here // row_devices
    inner_width = math.gcd(lax.axis_size("rows") * own_count, 512)
    inner_blocks = lax.axis_size("rows") * own_count // inner_width
    sub_src_blocks = sources.reshape(3, inner_blocks, inner_width).transpose(1, 0, 2)
    sub_wts_blocks = node_weight.reshape(inner_blocks, inner_width)

    def project_block(inputs):
        kernel_tile = kernel_cols(targets, inputs[0], inputs[1])
        return jnp.dot(kernel_tile, ortho_low, preferred_element_type=jnp.float32)

    projected = lax.psum_scatter(
        lax.map(project_block, (sub_src_blocks, sub_wts_blocks)).reshape(
            lax.axis_size("rows") * own_count, rank
        ),
        "rows",
        scatter_dimension=0,
        tiled=True,
    )
    scaled = ortho * math.sqrt(rows_here * row_devices)
    return (scaled, projected)


def solution(mesh):
    return jax.shard_map(
        shards,
        mesh=mesh,
        in_specs=(P(None, "rows"), P(None, "cols"), P("cols"), P("cols"), P("cols", None)),
        out_specs=(P("rows", None), P(("cols", "rows"), None)),
        check_vma=False,
    )
```

profile of v0, /device:TPU:8, one launch (start us, length us, event | category | flops | bytes accessed | tf_op | source)
XLA Modules:
  0.0 845.4 jit_solution(1076110894502836828)
XLA Ops:
  8.9 154.4 %while.22 = (s32[]{:T(128)}, f32[2048,128]{1,0:T(8,128)S(1)}, f32[8,512]{1,0:T(8,128)S(1)}, f32[3,2048]{1,0:T(4,128)}, f32[8,3,512]{2,1,0:T(4,128)}, /*index=5*/...) while((s32[]{:T(128)}, f32[2048,128]{1,0:T(8,128)S(1)}, f32[8,512]{1,0:T(8,128)S(1)}, ...), condition=%wide.region_1.2_spmd.clone, body=%wide.region_0.1_spmd.clone.sunk | while | flops 281543168 | bytes 2327191 | solution.py:63
  9.7 0.9 fusion.36
  10.6 17.5 %convolution_add_fusion.2 = f32[2048,128]{1,0:T(8,128)S(1)} fusion(f32[512]{0:T(512)S(1)} %bitcast.85, f32[2048]{0:T(1024)S(1)} %bitcast.77, f32[512]{0:T(512)S(1)} %bitcast.84, f32[2048]{0:T(1024)S(1)} %bitcast.78, f32[512]{0:T(512)S(1)} %bitcast.83, f32[2048]{0:T(1024)S(1)} %bitcast.76, f32[512]{0:T(512)S(1)} %bitcast.89, ...), kind=kOutput, calls=%fused_computation.10.clone.1 | convolution fusion | flops 281542656 | bytes 2261505 | tf_op jit(solution)/shard_map/while/body/eval_jaxpr/dot_general | solution.py:20
  29.0 0.9 fusion.36
  29.9 17.5 %convolution_add_fusion.2 = f32[2048,128]{1,0:T(8,128)S(1)} fusion(f32[512]{0:T(512)S(1)} %bitcast.85, f32[2048]{0:T(1024)S(1)} %bitcast.77, f32[512]{0:T(512)S(1)} %bitcast.84, f32[2048]{0:T(1024)S(1)} %bitcast.78, f32[512]{0:T(512)S(1)} %bitcast.83, f32[2048]{0:T(1024)S(1)} %bitcast.76, f32[512]{0:T(512)S(1)} %bitcast.89, ...), kind=kOutput, calls=%fused_computation.10.clone.1 | convolution fusion | flops 281542656 | bytes 2261505 | tf_op jit(solution)/shard_map/while/body/eval_jaxpr/dot_general | solution.py:20
  48.2 0.9 fusion.36
  49.1 17.5 %convolution_add_fusion.2 = f32[2048,128]{1,0:T(8,128)S(1)} fusion(f32[512]{0:T(512)S(1)} %bitcast.85, f32[2048]{0:T(1024)S(1)} %bitcast.77, f32[512]{0:T(512)S(1)} %bitcast.84, f32[2048]{0:T(1024)S(1)} %bitcast.78, f32[512]{0:T(512)S(1)} %bitcast.83, f32[2048]{0:T(1024)S(1)} %bitcast.76, f32[512]{0:T(512)S(1)} %bitcast.89, ...), kind=kOutput, calls=%fused_computation.10.clone.1 | convolution fusion | flops 281542656 | bytes 2261505 | tf_op jit(solution)/shard_map/while/body/eval_jaxpr/dot_general | solution.py:20
  67.5 0.9 fusion.36
  68.4 17.5 %convolution_add_fusion.2 = f32[2048,128]{1,0:T(8,128)S(1)} fusion(f32[512]{0:T(512)S(1)} %bitcast.85, f32[2048]{0:T(1024)S(1)} %bitcast.77, f32[512]{0:T(512)S(1)} %bitcast.84, f32[2048]{0:T(1024)S(1)} %bitcast.78, f32[512]{0:T(512)S(1)} %bitcast.83, f32[2048]{0:T(1024)S(1)} %bitcast.76, f32[512]{0:T(512)S(1)} %bitcast.89, ...), kind=kOutput, calls=%fused_computation.10.clone.1 | convolution fusion | flops 281542656 | bytes 2261505 | tf_op jit(solution)/shard_map/while/body/eval_jaxpr/dot_general | solution.py:20
  86.8 0.9 fusion.36
  87.7 17.5 %convolution_add_fusion.2 = f32[2048,128]{1,0:T(8,128)S(1)} fusion(f32[512]{0:T(512)S(1)} %bitcast.85, f32[2048]{0:T(1024)S(1)} %bitcast.77, f32[512]{0:T(512)S(1)} %bitcast.84, f32[2048]{0:T(1024)S(1)} %bitcast.78, f32[512]{0:T(512)S(1)} %bitcast.83, f32[2048]{0:T(1024)S(1)} %bitcast.76, f32[512]{0:T(512)S(1)} %bitcast.89, ...), kind=kOutput, calls=%fused_computation.10.clone.1 | convolution fusion | flops 281542656 | bytes 2261505 | tf_op jit(solution)/shard_map/while/body/eval_jaxpr/dot_general | solution.py:20
  107.0 17.5 %convolution_add_fusion.2 = f32[2048,128]{1,0:T(8,128)S(1)} fusion(f32[512]{0:T(512)S(1)} %bitcast.85, f32[2048]{0:T(1024)S(1)} %bitcast.77, f32[512]{0:T(512)S(1)} %bitcast.84, f32[2048]{0:T(1024)S(1)} %bitcast.78, f32[512]{0:T(512)S(1)} %bitcast.83, f32[2048]{0:T(1024)S(1)} %bitcast.76, f32[512]{0:T(512)S(1)} %bitcast.89, ...), kind=kOutput, calls=%fused_computation.10.clone.1 | convolution fusion | flops 281542656 | bytes 2261505 | tf_op jit(solution)/shard_map/while/body/eval_jaxpr/dot_general | solution.py:20
  126.3 17.5 %convolution_add_fusion.2 = f32[2048,128]{1,0:T(8,128)S(1)} fusion(f32[512]{0:T(512)S(1)} %bitcast.85, f32[2048]{0:T(1024)S(1)} %bitcast.77, f32[512]{0:T(512)S(1)} %bitcast.84, f32[2048]{0:T(1024)S(1)} %bitcast.78, f32[512]{0:T(512)S(1)} %bitcast.83, f32[2048]{0:T(1024)S(1)} %bitcast.76, f32[512]{0:T(512)S(1)} %bitcast.89, ...), kind=kOutput, calls=%fused_computation.10.clone.1 | convolution fusion | flops 281542656 | bytes 2261505 | tf_op jit(solution)/shard_map/while/body/eval_jaxpr/dot_general | solution.py:20
  145.5 17.5 %convolution_add_fusion.2 = f32[2048,128]{1,0:T(8,128)S(1)} fusion(f32[512]{0:T(512)S(1)} %bitcast.85, f32[2048]{0:T(1024)S(1)} %bitcast.77, f32[512]{0:T(512)S(1)} %bitcast.84, f32[2048]{0:T(1024)S(1)} %bitcast.78, f32[512]{0:T(512)S(1)} %bitcast.83, f32[2048]{0:T(1024)S(1)} %bitcast.76, f32[512]{0:T(512)S(1)} %bitcast.89, ...), kind=kOutput, calls=%fused_computation.10.clone.1 | convolution fusion | flops 281542656 | bytes 2261505 | tf_op jit(solution)/shard_map/while/body/eval_jaxpr/dot_general | solution.py:20
  163.3 1.0 copy-done.2
  164.3 120.4 %all-reduce.3.cloned.1.call-done = f32[2048,128]{1,0:T(8,128)} async-done(((f32[2048,128]{1,0:T(8,128)}), f32[2048,128]{1,0:T(8,128)}) %all-reduce.3.cloned.1.call-update) | async-done | bytes 1048592 | tf_op jit(solution)/shard_map/psum | solution.py:68
  284.7 4.1 fusion.22
  288.9 155.6 %all-reduce.5.cloned.1.call-done = f32[128,128]{0,1:T(8,128)} async-done(((f32[128,128]{0,1:T(8,128)}), f32[128,128]{0,1:T(8,128)}) %all-reduce.5.cloned.1.call-update) | async-done | bytes 65552 | tf_op jit(solution)/shard_map/psum | solution.py:69
  444.5 0.9 copy.10
  446.3 11.7 %cholesky.16 = f32[128,128]{1,0:T(8,128)S(1)} custom-call(f32[128,128]{1,0:T(8,128)S(1)} %fusion.18), custom_call_target="Cholesky" | custom-call | tf_op jit(solution)/shard_map/jit(cholesky)/cholesky | solution.py:35
  459.3 9.8 %custom-call.6 = f32[1,128,128]{1,2,0:T(8,128)S(1)} custom-call(f32[1,128,128]{2,1,0:T(8,128)S(1)} %fusion.15), custom_call_target="InvertDiagBlocksLowerTriangular" | custom-call | tf_op jit(solution)/shard_map/triangular_solve | solution.py:36
  469.2 1.9 fusion.21
  471.1 144.9 %while.21 = (s32[]{:T(128)}, f32[8,512,128]{2,1,0:T(8,128)}, f32[8,512]{1,0:T(8,128)S(1)}, f32[3,2048]{1,0:T(4,128)S(1)}, f32[8,3,512]{2,1,0:T(4,128)}, /*index=...) while((s32[]{:T(128)}, f32[8,512,128]{2,1,0:T(8,128)}, f32[8,512]{1,0:T(8,128)S(1)}, ...), condition=%wide.region_7.8_spmd, body=%wide.region_6.7_spmd.sunk | while | flops 281018880 | bytes 885389 | solution.py:84
  472.0 17.3 %fusion.34 = f32[8,512,128]{2,1,0:T(8,128)} fusion(f32[8,512,128]{2,1,0:T(8,128)} %get-tuple-element.266, s32[]{:T(128)} %get-tuple-element.265, bf16[2048,128]{1,0:T(8,128)(2,1)S(1)} %get-tuple-element.280, f32[512]{0:T(512)S(1)} %bitcast.88, f32[2048]{0:T(1024)S(1)} %bitcast.80, f32[512]{0:T(512)S(1)} %bitcast.87, f32[2048]{0:T(1024)S(1)} %bitcast.81, ...), kind=kOutput, calls=%fused_computation.3.clone.1 | convolution fusion | flops 281018368 | bytes 819712 | tf_op jit(solution)/shard_map/while/body/eval_jaxpr/dot_general | solution.py:81
  490.1 17.3 %fusion.34 = f32[8,512,128]{2,1,0:T(8,128)} fusion(f32[8,512,128]{2,1,0:T(8,128)} %get-tuple-element.266, s32[]{:T(128)} %get-tuple-element.265, bf16[2048,128]{1,0:T(8,128)(2,1)S(1)} %get-tuple-element.280, f32[512]{0:T(512)S(1)} %bitcast.88, f32[2048]{0:T(1024)S(1)} %bitcast.80, f32[512]{0:T(512)S(1)} %bitcast.87, f32[2048]{0:T(1024)S(1)} %bitcast.81, ...), kind=kOutput, calls=%fused_computation.3.clone.1 | convolution fusion | flops 281018368 | bytes 819712 | tf_op jit(solution)/shard_map/while/body/eval_jaxpr/dot_general | solution.py:81
  508.2 17.3 %fusion.34 = f32[8,512,128]{2,1,0:T(8,128)} fusion(f32[8,512,128]{2,1,0:T(8,128)} %get-tuple-element.266, s32[]{:T(128)} %get-tuple-element.265, bf16[2048,128]{1,0:T(8,128)(2,1)S(1)} %get-tuple-element.280, f32[512]{0:T(512)S(1)} %bitcast.88, f32[2048]{0:T(1024)S(1)} %bitcast.80, f32[512]{0:T(512)S(1)} %bitcast.87, f32[2048]{0:T(1024)S(1)} %bitcast.81, ...), kind=kOutput, calls=%fused_computation.3.clone.1 | convolution fusion | flops 281018368 | bytes 819712 | tf_op jit(solution)/shard_map/while/body/eval_jaxpr/dot_general | solution.py:81
  526.3 17.3 %fusion.34 = f32[8,512,128]{2,1,0:T(8,128)} fusion(f32[8,512,128]{2,1,0:T(8,128)} %get-tuple-element.266, s32[]{:T(128)} %get-tuple-element.265, bf16[2048,128]{1,0:T(8,128)(2,1)S(1)} %get-tuple-element.280, f32[512]{0:T(512)S(1)} %bitcast.88, f32[2048]{0:T(1024)S(1)} %bitcast.80, f32[512]{0:T(512)S(1)} %bitcast.87, f32[2048]{0:T(1024)S(1)} %bitcast.81, ...), kind=kOutput, calls=%fused_computation.3.clone.1 | convolution fusion | flops 281018368 | bytes 819712 | tf_op jit(solution)/shard_map/while/body/eval_jaxpr/dot_general | solution.py:81
  544.4 17.2 %fusion.34 = f32[8,512,128]{2,1,0:T(8,128)} fusion(f32[8,512,128]{2,1,0:T(8,128)} %get-tuple-element.266, s32[]{:T(128)} %get-tuple-element.265, bf16[2048,128]{1,0:T(8,128)(2,1)S(1)} %get-tuple-element.280, f32[512]{0:T(512)S(1)} %bitcast.88, f32[2048]{0:T(1024)S(1)} %bitcast.80, f32[512]{0:T(512)S(1)} %bitcast.87, f32[2048]{0:T(1024)S(1)} %bitcast.81, ...), kind=kOutput, calls=%fused_computation.3.clone.1 | convolution fusion | flops 281018368 | bytes 819712 | tf_op jit(solution)/shard_map/while/body/eval_jaxpr/dot_general | solution.py:81
  562.5 17.2 %fusion.34 = f32[8,512,128]{2,1,0:T(8,128)} fusion(f32[8,512,128]{2,1,0:T(8,128)} %get-tuple-element.266, s32[]{:T(128)} %get-tuple-element.265, bf16[2048,128]{1,0:T(8,128)(2,1)S(1)} %get-tuple-element.280, f32[512]{0:T(512)S(1)} %bitcast.88, f32[2048]{0:T(1024)S(1)} %bitcast.80, f32[512]{0:T(512)S(1)} %bitcast.87, f32[2048]{0:T(1024)S(1)} %bitcast.81, ...), kind=kOutput, calls=%fused_computation.3.clone.1 | convolution fusion | flops 281018368 | bytes 819712 | tf_op jit(solution)/shard_map/while/body/eval_jaxpr/dot_general | solution.py:81
  580.6 17.2 %fusion.34 = f32[8,512,128]{2,1,0:T(8,128)} fusion(f32[8,512,128]{2,1,0:T(8,128)} %get-tuple-element.266, s32[]{:T(128)} %get-tuple-element.265, bf16[2048,128]{1,0:T(8,128)(2,1)S(1)} %get-tuple-element.280, f32[512]{0:T(512)S(1)} %bitcast.88, f32[2048]{0:T(1024)S(1)} %bitcast.80, f32[512]{0:T(512)S(1)} %bitcast.87, f32[2048]{0:T(1024)S(1)} %bitcast.81, ...), kind=kOutput, calls=%fused_computation.3.clone.1 | convolution fusion | flops 281018368 | bytes 819712 | tf_op jit(solution)/shard_map/while/body/eval_jaxpr/dot_general | solution.py:81
  598.7 17.3 %fusion.34 = f32[8,512,128]{2,1,0:T(8,128)} fusion(f32[8,512,128]{2,1,0:T(8,128)} %get-tuple-element.266, s32[]{:T(128)} %get-tuple-element.265, bf16[2048,128]{1,0:T(8,128)(2,1)S(1)} %get-tuple-element.280, f32[512]{0:T(512)S(1)} %bitcast.88, f32[2048]{0:T(1024)S(1)} %bitcast.80, f32[512]{0:T(512)S(1)} %bitcast.87, f32[2048]{0:T(1024)S(1)} %bitcast.81, ...), kind=kOutput, calls=%fused_computation.3.clone.1 | convolution fusion | flops 281018368 | bytes 819712 | tf_op jit(solution)/shard_map/while/body/eval_jaxpr/dot_general | solution.py:81
  616.0 222.9 %reduce-scatter.2.cloned.1.call-done = f32[128,128]{1,0:T(8,128)} async-done(((f32[4096,128]{1,0:T(8,128)}), f32[128,128]{1,0:T(8,128)}) %reduce-scatter.2.cloned.1.call-update) | async-done | bytes 65552 | tf_op jit(solution)/shard_map/reduce_scatter | solution.py:83
  (64 shorter events, 20.0 us)
Async XLA Ops:
  7.2 277.5 %all-reduce.3.cloned.1.call-start = ((), (), s32[]{:S(2)}) async-start(), calls=%async_computation.1 | async-start | bytes 2097152 | tf_op jit(solution)/shard_map/psum | solution.py:68
  163.3 1.0 copy-start.2
  164.3 280.2 %all-reduce.5.cloned.1.call-start = ((), (), s32[]{:S(2)}) async-start(), calls=%async_computation.2 | async-start | bytes 131072 | tf_op jit(solution)/shard_map/psum | solution.py:69
  284.7 184.5 %copy-start = (f32[2048,128]{1,0:T(8,128)S(1)}, f32[2048,128]{1,0:T(8,128)}, u32[]{:S(2)}) copy-start(f32[2048,128]{1,0:T(8,128)} %all-reduce.3.cloned.1.call-done) | copy-start | bytes 3145732
  288.8 182.3 %copy-start.1 = (f32[3,2048]{1,0:T(4,128)S(1)}, f32[3,2048]{1,0:T(4,128)}, u32[]{:S(2)}) copy-start(f32[3,2048]{1,0:T(4,128)} %get-tuple-element.291) | copy-start | bytes 73732
  288.8 550.0 %reduce-scatter.2.cloned.1.call-start = ((), (), s32[]{:S(2)}) async-start(), calls=%async_computation.3 | async-start | bytes 2162688 | tf_op jit(solution)/shard_map/reduce_scatter | solution.py:83
Sparse Core Ops, SparseCore 0:
  164.4 120.2 all-reduce.2
  289.0 155.4 all-reduce.4
  616.1 222.6 reduce-scatter.1
where the time goes:
time: 847 us; the launch traced here: 845 us
  waiting for transfers between devices  499 us (59%)
  matrix products  284 us (34%)
  other arithmetic  38.3 us (5%)
  between operations  13.8 us (2%)
  local copies, waits for them, and re-layouts  9.44 us (1%)
    reduce_scatter x1, waiting for transfers between devices, shards(): lax.psum_scatter(lax.map(project_block, (sub_src_blocks, sub_wts_blocks))...  223 us
    psum x1, waiting for transfers between devices, shards(): gram_matrix = lax.psum(gram_of(sketch), 'rows')  156 us
    dot_general x8, matrix products, contract_first(): lax.dot_general(left, right, (((0,), (0,)), ((), ())), preferred_element_...  140 us
    dot_general x8, matrix products, project_block(): return jnp.dot(kernel_tile, ortho_low, preferred_element_type=jnp.float32)  138 us
    psum x1, waiting for transfers between devices, shards(): sketch = lax.psum(partial_sketch, 'cols')  120 us
  transfers between devices with their start and end apart: 3, of which 3 were waited for; matrix products, arithmetic and copies ran while one was open for 0% of the time, Pallas kernels for 0%

commit v1 on v0

--- a/solution.py
+++ b/solution.py
@@ -6,6 +6,16 @@
 
 wave_number = 160.0
 separation = 2.0
+
+
+def clear_tasks(chunk):
+    n_slots = lax.psum(1, "cols")
+    base_arr = chunk
+    for to_i in [nth for nth in (1, 2, 4, 8, 16) if nth < n_slots]:
+        base_arr = base_arr + lax.ppermute(
+            base_arr, "cols", perm=tuple(((pp, pp ^ to_i) for pp in range(n_slots)))
+        )
+    return base_arr
 
 
 def kernel_cols(targets, src_block, wts_block):
@@ -65,7 +75,7 @@
         jnp.zeros((rows_here, rank), jnp.float32),
         (src_blocks, wts_blocks, omega_blocks),
     )
-    sketch = lax.psum(partial_sketch, "cols")
+    sketch = clear_tasks(partial_sketch)
     gram_matrix = lax.psum(gram_of(sketch), "rows")
     ortho = solve_rows(sketch, gram_matrix)
     ortho_low = ortho.astype(jnp.bfloat16)

time: 847 us -> 879 us (1.038); the launches traced: 845 us -> 865 us
  starting transfers between devices: 0.12 us -> 14.6 us
    psum x1 -> x0, waiting for transfers between devices: 120 us -> none  [shards(): sketch = lax.psum(partial_sketch, 'cols')]
    ppermute x0 -> x4, waiting for transfers between devices: none -> 109 us  [clear_tasks(): lax.ppermute(base_arr, 'cols', perm=tuple(((pp, pp ^ to_i) for pp in rang...]
    ppermute x0 -> x4, starting transfers between devices: none -> 14.5 us  [clear_tasks(): lax.ppermute(base_arr, 'cols', perm=tuple(((pp, pp ^ to_i) for pp in rang...]
    psum x1, waiting for transfers between devices: 156 us -> 166 us  [shards(): gram_matrix = lax.psum(gram_of(sketch), 'rows')]
  transfers between devices with their start and end apart: 3 -> 6, of which waited for: 3 -> 6; matrix products, arithmetic and copies ran while one was open for 0% -> 0% of each run, Pallas kernels for 0% -> 0%
where the time goes in v1:
time: 879 us; the launch traced here: 865 us
  waiting for transfers between devices  498 us (57%)
  matrix products  283 us (32%)
  other arithmetic  38.7 us (4%)
  starting transfers between devices  14.6 us (2%)
  between operations  14.5 us (2%)
    reduce_scatter x1, waiting for transfers between devices, shards(): lax.psum_scatter(lax.map(project_block, (sub_src_blocks, sub_wts_blocks))...  223 us
    psum x1, waiting for transfers between devices, shards(): gram_matrix = lax.psum(gram_of(sketch), 'rows')  166 us
    dot_general x8, matrix products, contract_first(): lax.dot_general(left, right, (((0,), (0,)), ((), ())), preferred_element_...  140 us
    dot_general x8, matrix products, project_block(): return jnp.dot(kernel_tile, ortho_low, preferred_element_type=jnp.float32)  138 us
    ppermute x4, waiting for transfers between devices, clear_tasks(): lax.ppermute(base_arr, 'cols', perm=tuple(((pp, pp ^ to_i) for pp in rang...  109 us
  transfers between devices with their start and end apart: 6, of which 6 were waited for; matrix products, arithmetic and copies ran while one was open for 0% of the time, Pallas kernels for 0%

profile of v1, /device:TPU:8, one launch (start us, length us, event | category | flops | bytes accessed | tf_op | source)
XLA Modules:
  0.0 864.9 jit_solution(2708519385734616404)
XLA Ops:
  8.9 161.8 %while.22 = (s32[]{:T(128)}, f32[2048,128]{1,0:T(8,128)S(1)}, f32[8,512]{1,0:T(8,128)S(1)}, f32[3,2048]{1,0:T(4,128)}, f32[8,3,512]{2,1,0:T(4,128)}, /*index=5*/...) while((s32[]{:T(128)}, f32[2048,128]{1,0:T(8,128)S(1)}, f32[8,512]{1,0:T(8,128)S(1)}, ...), condition=%wide.region_1.2_spmd.clone, body=%wide.region_0.1_spmd.clone.sunk | while | flops 281543168 | bytes 2327191 | solution.py:73
  10.6 17.5 %convolution_add_fusion.2 = f32[2048,128]{1,0:T(8,128)S(1)} fusion(f32[512]{0:T(512)S(1)} %bitcast.85, f32[2048]{0:T(1024)S(1)} %bitcast.77, f32[512]{0:T(512)S(1)} %bitcast.84, f32[2048]{0:T(1024)S(1)} %bitcast.78, f32[512]{0:T(512)S(1)} %bitcast.83, f32[2048]{0:T(1024)S(1)} %bitcast.76, f32[512]{0:T(512)S(1)} %bitcast.89, ...), kind=kOutput, calls=%fused_computation.10.clone.1 | convolution fusion | flops 281542656 | bytes 2261505 | tf_op jit(solution)/shard_map/while/body/eval_jaxpr/dot_general | solution.py:30
  29.9 17.5 %convolution_add_fusion.2 = f32[2048,128]{1,0:T(8,128)S(1)} fusion(f32[512]{0:T(512)S(1)} %bitcast.85, f32[2048]{0:T(1024)S(1)} %bitcast.77, f32[512]{0:T(512)S(1)} %bitcast.84, f32[2048]{0:T(1024)S(1)} %bitcast.78, f32[512]{0:T(512)S(1)} %bitcast.83, f32[2048]{0:T(1024)S(1)} %bitcast.76, f32[512]{0:T(512)S(1)} %bitcast.89, ...), kind=kOutput, calls=%fused_computation.10.clone.1 | convolution fusion | flops 281542656 | bytes 2261505 | tf_op jit(solution)/shard_map/while/body/eval_jaxpr/dot_general | solution.py:30
  49.1 17.5 %convolution_add_fusion.2 = f32[2048,128]{1,0:T(8,128)S(1)} fusion(f32[512]{0:T(512)S(1)} %bitcast.85, f32[2048]{0:T(1024)S(1)} %bitcast.77, f32[512]{0:T(512)S(1)} %bitcast.84, f32[2048]{0:T(1024)S(1)} %bitcast.78, f32[512]{0:T(512)S(1)} %bitcast.83, f32[2048]{0:T(1024)S(1)} %bitcast.76, f32[512]{0:T(512)S(1)} %bitcast.89, ...), kind=kOutput, calls=%fused_computation.10.clone.1 | convolution fusion | flops 281542656 | bytes 2261505 | tf_op jit(solution)/shard_map/while/body/eval_jaxpr/dot_general | solution.py:30
  68.4 17.5 %convolution_add_fusion.2 = f32[2048,128]{1,0:T(8,128)S(1)} fusion(f32[512]{0:T(512)S(1)} %bitcast.85, f32[2048]{0:T(1024)S(1)} %bitcast.77, f32[512]{0:T(512)S(1)} %bitcast.84, f32[2048]{0:T(1024)S(1)} %bitcast.78, f32[512]{0:T(512)S(1)} %bitcast.83, f32[2048]{0:T(1024)S(1)} %bitcast.76, f32[512]{0:T(512)S(1)} %bitcast.89, ...), kind=kOutput, calls=%fused_computation.10.clone.1 | convolution fusion | flops 281542656 | bytes 2261505 | tf_op jit(solution)/shard_map/while/body/eval_jaxpr/dot_general | solution.py:30
  87.7 17.5 %convolution_add_fusion.2 = f32[2048,128]{1,0:T(8,128)S(1)} fusion(f32[512]{0:T(512)S(1)} %bitcast.85, f32[2048]{0:T(1024)S(1)} %bitcast.77, f32[512]{0:T(512)S(1)} %bitcast.84, f32[2048]{0:T(1024)S(1)} %bitcast.78, f32[512]{0:T(512)S(1)} %bitcast.83, f32[2048]{0:T(1024)S(1)} %bitcast.76, f32[512]{0:T(512)S(1)} %bitcast.89, ...), kind=kOutput, calls=%fused_computation.10.clone.1 | convolution fusion | flops 281542656 | bytes 2261505 | tf_op jit(solution)/shard_map/while/body/eval_jaxpr/dot_general | solution.py:30
  107.0 17.5 %convolution_add_fusion.2 = f32[2048,128]{1,0:T(8,128)S(1)} fusion(f32[512]{0:T(512)S(1)} %bitcast.85, f32[2048]{0:T(1024)S(1)} %bitcast.77, f32[512]{0:T(512)S(1)} %bitcast.84, f32[2048]{0:T(1024)S(1)} %bitcast.78, f32[512]{0:T(512)S(1)} %bitcast.83, f32[2048]{0:T(1024)S(1)} %bitcast.76, f32[512]{0:T(512)S(1)} %bitcast.89, ...), kind=kOutput, calls=%fused_computation.10.clone.1 | convolution fusion | flops 281542656 | bytes 2261505 | tf_op jit(solution)/shard_map/while/body/eval_jaxpr/dot_general | solution.py:30
  126.3 17.5 %convolution_add_fusion.2 = f32[2048,128]{1,0:T(8,128)S(1)} fusion(f32[512]{0:T(512)S(1)} %bitcast.85, f32[2048]{0:T(1024)S(1)} %bitcast.77, f32[512]{0:T(512)S(1)} %bitcast.84, f32[2048]{0:T(1024)S(1)} %bitcast.78, f32[512]{0:T(512)S(1)} %bitcast.83, f32[2048]{0:T(1024)S(1)} %bitcast.76, f32[512]{0:T(512)S(1)} %bitcast.89, ...), kind=kOutput, calls=%fused_computation.10.clone.1 | convolution fusion | flops 281542656 | bytes 2261505 | tf_op jit(solution)/shard_map/while/body/eval_jaxpr/dot_general | solution.py:30
  145.5 17.5 %convolution_add_fusion.2 = f32[2048,128]{1,0:T(8,128)S(1)} fusion(f32[512]{0:T(512)S(1)} %bitcast.85, f32[2048]{0:T(1024)S(1)} %bitcast.77, f32[512]{0:T(512)S(1)} %bitcast.84, f32[2048]{0:T(1024)S(1)} %bitcast.78, f32[512]{0:T(512)S(1)} %bitcast.83, f32[2048]{0:T(1024)S(1)} %bitcast.76, f32[512]{0:T(512)S(1)} %bitcast.89, ...), kind=kOutput, calls=%fused_computation.10.clone.1 | convolution fusion | flops 281542656 | bytes 2261505 | tf_op jit(solution)/shard_map/while/body/eval_jaxpr/dot_general | solution.py:30
  170.7 1.9 collective-permute-start
  172.6 2.6 collective-permute-done
  175.3 7.7 collective-permute-start.1
  183.0 23.4 %collective-permute-done.1 = f32[2048,128]{1,0:T(8,128)S(1)} collective-permute-done((f32[2048,128]{1,0:T(8,128)S(1)}, f32[2048,128]{1,0:T(8,128)S(1)}, u32[]{:S(2)}, u32[]{:S(2)}) %collective-permute-start.1) | collective-permute-done | bytes 1048608 | tf_op jit(solution)/shard_map/ppermute | solution.py:15
  206.6 1.9 collective-permute-start.2
  208.5 44.9 %collective-permute-done.2 = f32[2048,128]{1,0:T(8,128)S(1)} collective-permute-done((f32[2048,128]{1,0:T(8,128)S(1)}, f32[2048,128]{1,0:T(8,128)S(1)}, u32[]{:S(2)}, u32[]{:S(2)}) %collective-permute-start.2) | collective-permute-done | bytes 1048608 | tf_op jit(solution)/shard_map/ppermute | solution.py:15
  253.5 3.0 collective-permute-start.3
  256.5 37.8 %collective-permute-done.3 = f32[2048,128]{1,0:T(8,128)S(1)} collective-permute-done((f32[2048,128]{1,0:T(8,128)S(1)}, f32[2048,128]{1,0:T(8,128)S(1)}, u32[]{:S(2)}, u32[]{:S(2)}) %collective-permute-start.3) | collective-permute-done | bytes 1048608 | tf_op jit(solution)/shard_map/ppermute | solution.py:15
  294.5 2.4 fusion.22
  297.0 166.3 %all-reduce.2.cloned.1.call-done = f32[128,128]{0,1:T(8,128)} async-done(((f32[128,128]{0,1:T(8,128)}), f32[128,128]{0,1:T(8,128)}) %all-reduce.2.cloned.1.call-update) | async-done | bytes 65552 | tf_op jit(solution)/shard_map/psum | solution.py:79
  465.1 11.7 %cholesky.16 = f32[128,128]{1,0:T(8,128)S(1)} custom-call(f32[128,128]{1,0:T(8,128)S(1)} %fusion.18), custom_call_target="Cholesky" | custom-call | tf_op jit(solution)/shard_map/jit(cholesky)/cholesky | solution.py:45
  478.1 9.8 %custom-call.6 = f32[1,128,128]{1,2,0:T(8,128)S(1)} custom-call(f32[1,128,128]{2,1,0:T(8,128)S(1)} %fusion.15), custom_call_target="InvertDiagBlocksLowerTriangular" | custom-call | tf_op jit(solution)/shard_map/triangular_solve | solution.py:46
  488.0 1.9 fusion.21
  489.9 144.9 %while.21 = (s32[]{:T(128)}, f32[8,512,128]{2,1,0:T(8,128)}, f32[8,512]{1,0:T(8,128)S(1)}, f32[3,2048]{1,0:T(4,128)S(1)}, f32[8,3,512]{2,1,0:T(4,128)}, /*index=...) while((s32[]{:T(128)}, f32[8,512,128]{2,1,0:T(8,128)}, f32[8,512]{1,0:T(8,128)S(1)}, ...), condition=%wide.region_6.7_spmd, body=%wide.region_5.6_spmd.sunk | while | flops 281018880 | bytes 885389 | solution.py:94
  490.8 17.3 %fusion.34 = f32[8,512,128]{2,1,0:T(8,128)} fusion(f32[8,512,128]{2,1,0:T(8,128)} %get-tuple-element.266, s32[]{:T(128)} %get-tuple-element.265, bf16[2048,128]{1,0:T(8,128)(2,1)S(1)} %get-tuple-element.280, f32[512]{0:T(512)S(1)} %bitcast.88, f32[2048]{0:T(1024)S(1)} %bitcast.80, f32[512]{0:T(512)S(1)} %bitcast.87, f32[2048]{0:T(1024)S(1)} %bitcast.81, ...), kind=kOutput, calls=%fused_computation.3.clone.1 | convolution fusion | flops 281018368 | bytes 819712 | tf_op jit(solution)/shard_map/while/body/eval_jaxpr/dot_general | solution.py:91
  508.9 17.3 %fusion.34 = f32[8,512,128]{2,1,0:T(8,128)} fusion(f32[8,512,128]{2,1,0:T(8,128)} %get-tuple-element.266, s32[]{:T(128)} %get-tuple-element.265, bf16[2048,128]{1,0:T(8,128)(2,1)S(1)} %get-tuple-element.280, f32[512]{0:T(512)S(1)} %bitcast.88, f32[2048]{0:T(1024)S(1)} %bitcast.80, f32[512]{0:T(512)S(1)} %bitcast.87, f32[2048]{0:T(1024)S(1)} %bitcast.81, ...), kind=kOutput, calls=%fused_computation.3.clone.1 | convolution fusion | flops 281018368 | bytes 819712 | tf_op jit(solution)/shard_map/while/body/eval_jaxpr/dot_general | solution.py:91
  527.0 17.3 %fusion.34 = f32[8,512,128]{2,1,0:T(8,128)} fusion(f32[8,512,128]{2,1,0:T(8,128)} %get-tuple-element.266, s32[]{:T(128)} %get-tuple-element.265, bf16[2048,128]{1,0:T(8,128)(2,1)S(1)} %get-tuple-element.280, f32[512]{0:T(512)S(1)} %bitcast.88, f32[2048]{0:T(1024)S(1)} %bitcast.80, f32[512]{0:T(512)S(1)} %bitcast.87, f32[2048]{0:T(1024)S(1)} %bitcast.81, ...), kind=kOutput, calls=%fused_computation.3.clone.1 | convolution fusion | flops 281018368 | bytes 819712 | tf_op jit(solution)/shard_map/while/body/eval_jaxpr/dot_general | solution.py:91
  545.1 17.3 %fusion.34 = f32[8,512,128]{2,1,0:T(8,128)} fusion(f32[8,512,128]{2,1,0:T(8,128)} %get-tuple-element.266, s32[]{:T(128)} %get-tuple-element.265, bf16[2048,128]{1,0:T(8,128)(2,1)S(1)} %get-tuple-element.280, f32[512]{0:T(512)S(1)} %bitcast.88, f32[2048]{0:T(1024)S(1)} %bitcast.80, f32[512]{0:T(512)S(1)} %bitcast.87, f32[2048]{0:T(1024)S(1)} %bitcast.81, ...), kind=kOutput, calls=%fused_computation.3.clone.1 | convolution fusion | flops 281018368 | bytes 819712 | tf_op jit(solution)/shard_map/while/body/eval_jaxpr/dot_general | solution.py:91
  563.2 17.3 %fusion.34 = f32[8,512,128]{2,1,0:T(8,128)} fusion(f32[8,512,128]{2,1,0:T(8,128)} %get-tuple-element.266, s32[]{:T(128)} %get-tuple-element.265, bf16[2048,128]{1,0:T(8,128)(2,1)S(1)} %get-tuple-element.280, f32[512]{0:T(512)S(1)} %bitcast.88, f32[2048]{0:T(1024)S(1)} %bitcast.80, f32[512]{0:T(512)S(1)} %bitcast.87, f32[2048]{0:T(1024)S(1)} %bitcast.81, ...), kind=kOutput, calls=%fused_computation.3.clone.1 | convolution fusion | flops 281018368 | bytes 819712 | tf_op jit(solution)/shard_map/while/body/eval_jaxpr/dot_general | solution.py:91
  581.3 17.3 %fusion.34 = f32[8,512,128]{2,1,0:T(8,128)} fusion(f32[8,512,128]{2,1,0:T(8,128)} %get-tuple-element.266, s32[]{:T(128)} %get-tuple-element.265, bf16[2048,128]{1,0:T(8,128)(2,1)S(1)} %get-tuple-element.280, f32[512]{0:T(512)S(1)} %bitcast.88, f32[2048]{0:T(1024)S(1)} %bitcast.80, f32[512]{0:T(512)S(1)} %bitcast.87, f32[2048]{0:T(1024)S(1)} %bitcast.81, ...), kind=kOutput, calls=%fused_computation.3.clone.1 | convolution fusion | flops 281018368 | bytes 819712 | tf_op jit(solution)/shard_map/while/body/eval_jaxpr/dot_general | solution.py:91
  599.4 17.2 %fusion.34 = f32[8,512,128]{2,1,0:T(8,128)} fusion(f32[8,512,128]{2,1,0:T(8,128)} %get-tuple-element.266, s32[]{:T(128)} %get-tuple-element.265, bf16[2048,128]{1,0:T(8,128)(2,1)S(1)} %get-tuple-element.280, f32[512]{0:T(512)S(1)} %bitcast.88, f32[2048]{0:T(1024)S(1)} %bitcast.80, f32[512]{0:T(512)S(1)} %bitcast.87, f32[2048]{0:T(1024)S(1)} %bitcast.81, ...), kind=kOutput, calls=%fused_computation.3.clone.1 | convolution fusion | flops 281018368 | bytes 819712 | tf_op jit(solution)/shard_map/while/body/eval_jaxpr/dot_general | solution.py:91
  617.5 17.3 %fusion.34 = f32[8,512,128]{2,1,0:T(8,128)} fusion(f32[8,512,128]{2,1,0:T(8,128)} %get-tuple-element.266, s32[]{:T(128)} %get-tuple-element.265, bf16[2048,128]{1,0:T(8,128)(2,1)S(1)} %get-tuple-element.280, f32[512]{0:T(512)S(1)} %bitcast.88, f32[2048]{0:T(1024)S(1)} %bitcast.80, f32[512]{0:T(512)S(1)} %bitcast.87, f32[2048]{0:T(1024)S(1)} %bitcast.81, ...), kind=kOutput, calls=%fused_computation.3.clone.1 | convolution fusion | flops 281018368 | bytes 819712 | tf_op jit(solution)/shard_map/while/body/eval_jaxpr/dot_general | solution.py:91
  634.8 222.9 %reduce-scatter.2.cloned.1.call-done = f32[128,128]{1,0:T(8,128)} async-done(((f32[4096,128]{1,0:T(8,128)}), f32[128,128]{1,0:T(8,128)}) %reduce-scatter.2.cloned.1.call-update) | async-done | bytes 65552 | tf_op jit(solution)/shard_map/reduce_scatter | solution.py:93
  (69 shorter events, 25.8 us)
Async XLA Ops:
  7.2 456.1 %all-reduce.2.cloned.1.call-start = ((), (), s32[]{:S(2)}) async-start(), calls=%async_computation.1 | async-start | bytes 131072 | tf_op jit(solution)/shard_map/psum | solution.py:79
  170.7 4.6 collective-permute-start
  175.3 31.2 %collective-permute-start.1 = (f32[2048,128]{1,0:T(8,128)S(1)}, f32[2048,128]{1,0:T(8,128)S(1)}, u32[]{:S(2)}, u32[]{:S(2)}) collective-permute-start(f32[2048,128]{1,0:T(8,128)S(1)} %add.70), channel_id=1, source_target_pairs={{0,2},{1,3},{2,0},{3,1},{4,6},{5,7},{6,4},{7,5},{8,10},{9,11},{10,... | collective-permute-start | bytes 3145736 | tf_op jit(solution)/shard_map/ppermute | solution.py:15
  206.6 46.8 %collective-permute-start.2 = (f32[2048,128]{1,0:T(8,128)S(1)}, f32[2048,128]{1,0:T(8,128)S(1)}, u32[]{:S(2)}, u32[]{:S(2)}) collective-permute-start(f32[2048,128]{1,0:T(8,128)S(1)} %add.71), channel_id=1, source_target_pairs={{0,4},{1,5},{2,6},{3,7},{4,0},{5,1},{6,2},{7,3},{8,12},{9,13},{10,... | collective-permute-start | bytes 3145736 | tf_op jit(solution)/shard_map/ppermute | solution.py:15
  253.5 40.8 %collective-permute-start.3 = (f32[2048,128]{1,0:T(8,128)S(1)}, f32[2048,128]{1,0:T(8,128)S(1)}, u32[]{:S(2)}, u32[]{:S(2)}) collective-permute-start(f32[2048,128]{1,0:T(8,128)S(1)} %add.72), channel_id=1, source_target_pairs={{0,8},{1,9},{2,10},{3,11},{4,12},{5,13},{6,14},{7,15},{8,0},{9,1},... | collective-permute-start | bytes 3145736 | tf_op jit(solution)/shard_map/ppermute | solution.py:15
  296.9 193.0 %copy-start = (f32[3,2048]{1,0:T(4,128)S(1)}, f32[3,2048]{1,0:T(4,128)}, u32[]{:S(2)}) copy-start(f32[3,2048]{1,0:T(4,128)} %get-tuple-element.292) | copy-start | bytes 73732
  296.9 560.7 %reduce-scatter.2.cloned.1.call-start = ((), (), s32[]{:S(2)}) async-start(), calls=%async_computation.2 | async-start | bytes 2162688 | tf_op jit(solution)/shard_map/reduce_scatter | solution.py:93
Sparse Core Ops, SparseCore 0:
  297.1 166.1 all-reduce.1
  634.9 222.6 reduce-scatter.1
